TPU v7x, 256 devices: a whole 4x4x8 slice. The times are simulated.
256 devices in a mesh: row: 32 (over x, z_hi, core), col: 8 (over y, z_lo).
Axes of the slice: x: 4, y: 4, z: 8 (z_hi: 4, z_lo: 2; z = z_hi * 2 + z_lo), core: 2. Of those that a mesh axis runs over, the one named last changes fastest.
Arguments:
- sigma_anc: float32 [128, 128, 128, 128], P('row', 'col'), as said below
- panel: float32 [2, 128, 128, 512], P(None, 'row'), may hold values from -0.12 to 0.12
- pattern: int32 [2, 64], replicated, may hold values from 0 to 127, as said below
- linv: float32 [2, 512, 512], replicated, as said below
Outputs:
- sigma_sj: float32 [2, 128, 128, 512], P(None, 'row')
- sigma_jj: float32 [2, 512, 512], replicated
Inputs may be any that keep to these rules, and one draw needn't show every extreme that they name: `pattern`: each row lists 64 distinct ancestor block indices in increasing order; 0 and 127 are always among them. `sigma_anc`: symmetric as a matrix of order 128 * 128 in ancestor order. `linv`: lower triangular, diagonal entries between 1 and 2.
All inputs are finite; a program needn't handle non-finite values.
Results may differ from a plain program's by a relative error of at most 0.0001.
Values sent between devices are 32-bit elements; how exact they have to be, the bound alone decides.
A program may use at most 128 MiB of HBM per device.

v0:
```python
import jax
import jax.numpy as jnp
from jax import lax
from jax.sharding import PartitionSpec as P


def local(sigma_anc, panel, pattern, linv):
    highest = lax.Precision.HIGHEST
    rows_here = sigma_anc.shape[0]
    cols_here = sigma_anc.shape[1]
    row_count = lax.axis_size("row")
    col_count = lax.axis_size("col")
    row_index = lax.axis_index("row")
    column_index = lax.axis_index("col")
    row_ids = jnp.arange(rows_here, dtype=jnp.int32) * row_count + row_index
    col_ids = jnp.arange(cols_here, dtype=jnp.int32) * col_count + column_index
    in_pattern = jnp.any(pattern[:, :, None] == row_ids[None, None, :], axis=1).astype(jnp.float32)
    updated = jnp.einsum(
        "sqiw,swv->sqiv", panel, linv, precision=highest, preferred_element_type=jnp.float32
    )
    updated = updated * in_pattern[:, :, None, None]
    selector = (col_ids[:, None] == row_ids[None, :]).astype(jnp.float32)
    local_cols = jnp.einsum(
        "kq,sqiw->skiw", selector, updated, precision=highest, preferred_element_type=jnp.float32
    )
    gathered_cols = lax.psum(local_cols, "row")
    partial_value = jnp.einsum(
        "qkij,skjw->sqiw",
        sigma_anc,
        gathered_cols,
        precision=highest,
        preferred_element_type=jnp.float32,
    )
    product = lax.psum(partial_value, "col")
    product = product * in_pattern[:, :, None, None]
    sigma_sj = -product
    base_term = jnp.einsum(
        "siw,siv->swv", linv, linv, precision=highest, preferred_element_type=jnp.float32
    )
    local_term = jnp.einsum(
        "sqiw,sqiv->swv", updated, product, precision=highest, preferred_element_type=jnp.float32
    )
    total_term = lax.psum(local_term, "row")
    sigma_jj = base_term + total_term
    return (sigma_sj, sigma_jj)


def solution(mesh):
    return jax.shard_map(
        local,
        mesh=mesh,
        in_specs=(P("row", "col", None, None), P(None, "row", None, None), P(), P()),
        out_specs=(P(None, "row", None, None), P()),
        check_vma=False,
    )
```

profile of v0, /device:TPU:1, one launch (start us, length us, event | category | flops | bytes accessed | tf_op | source)
XLA Modules:
  0.0 793.9 jit_solution(9738361498573340036)
XLA Ops:
  7.2 0.0 copy-start
  7.2 0.0 all-reduce.4.cloned.1.call-start
  7.3 1.0 compare_reduce_fusion
  8.3 0.5 copy-done
  8.8 5.1 fusion.12
  13.9 0.0 copy-start.1
  13.9 1.3 copy-done.1
  15.2 6.0 fusion.5
  21.2 10.0 %copy.15 = f32[2,128,512,16]{1,2,3,0:T(8,128)} copy(f32[2,128,512,16]{2,3,1,0:T(8,128)} %fusion.5) | data formatting | bytes 16777216 | tf_op jit(solution)/shard_map/kq,sqiw->skiw/dot_general | solution.py:23
  31.2 0.0 all-reduce.4.cloned.1.call-update
  31.2 0.2 all-reduce.6.cloned.1.call-start
  31.5 328.1 %all-reduce.4.cloned.1.call-done = f32[2,16,128,512]{2,3,1,0:T(8,128)} async-done(((f32[2,16,128,512]{2,3,1,0:T(8,128)}), f32[2,16,128,512]{2,3,1,0:T(8,128)}) %all-reduce.4.cloned.1.call-update) | async-done | bytes 8388624 | tf_op jit(solution)/shard_map/psum | solution.py:26
  359.6 17.7 %fusion.15 = f32[2,4,128,512]{3,2,1,0:T(8,128)} fusion(f32[4,16,128,128]{3,2,1,0:T(8,128)} %param.4, f32[2,16,128,512]{2,3,1,0:T(8,128)} %all-reduce.4.cloned.1.call-done), kind=kOutput, calls=%fused_computation.12 | convolution fusion | flops 12884901888 | bytes 14680064 | tf_op jit(solution)/shard_map/qkij,skjw->sqiw/dot_general | solution.py:27
  377.3 0.0 all-reduce.6.cloned.1.call-update
  377.4 0.3 all-reduce.8.cloned.1.call-start
  377.6 107.8 %all-reduce.6.cloned.1.call-done = f32[2,4,128,512]{3,2,1,0:T(8,128)} async-done(((f32[2,4,128,512]{3,2,1,0:T(8,128)}), f32[2,4,128,512]{3,2,1,0:T(8,128)}) %all-reduce.6.cloned.1.call-update) | async-done | bytes 2097168 | tf_op jit(solution)/shard_map/psum | solution.py:34
  485.4 7.4 fusion.9
  492.8 0.0 all-reduce.8.cloned.1.call-update
  492.8 3.4 multiply_negate_fusion
  496.2 285.3 %all-reduce.8.cloned.1.call-done = f32[2,512,512]{2,1,0:T(8,128)} async-done(((f32[2,512,512]{2,1,0:T(8,128)}), f32[2,512,512]{2,1,0:T(8,128)}) %all-reduce.8.cloned.1.call-update) | async-done | bytes 2097168 | tf_op jit(solution)/shard_map/psum | solution.py:43
  781.4 5.9 convolution_add_fusion
  (3 shorter events, 0.0 us)
Async XLA Ops:
  7.2 1.6 copy-start
  7.2 352.4 %all-reduce.4.cloned.1.call-start = ((), (), s32[]{:S(2)}) async-start(), calls=%async_computation | async-start | bytes 16777216 | tf_op jit(solution)/shard_map/psum | solution.py:26
  13.9 1.3 copy-start.1
  31.2 454.2 %all-reduce.6.cloned.1.call-start = ((), (), s32[]{:S(2)}) async-start(), calls=%async_computation.1 | async-start | bytes 4194304 | tf_op jit(solution)/shard_map/psum | solution.py:34
  377.4 404.1 %all-reduce.8.cloned.1.call-start = ((), (), s32[]{:S(2)}) async-start(), calls=%async_computation.2 | async-start | bytes 4194304 | tf_op jit(solution)/shard_map/psum | solution.py:43
Sparse Core Ops, SparseCore 0:
  31.4 328.1 all-reduce.3
  377.5 107.8 all-reduce.5
  492.9 288.4 all-reduce.7
where the time goes:
time: 794 us
  waiting for transfers between devices  721 us (91%)
  matrix products  42.1 us (5%)
  between operations  13.8 us (2%)
  local copies, waits for them, and re-layouts  11.9 us (1%)
    psum x1, waiting for transfers between devices, local(): gathered_cols = lax.psum(local_cols, 'row')  328 us
    psum x1, waiting for transfers between devices, local(): total_term = lax.psum(local_term, 'row')  285 us
    psum x1, waiting for transfers between devices, local(): product = lax.psum(partial_value, 'col')  108 us
    dot_general x1, matrix products, local(): jnp.einsum('qkij,skjw->sqiw', sigma_anc, gathered_cols, precision=highest...  17.7 us
  transfers between devices with their start and end apart: 3, of which 3 were waited for; matrix products, arithmetic and copies ran while one was open for 0% of the time, Pallas kernels for 0%

commit v1 on v0

v1 whole, which is shorter than its diff:
```python
import jax
import jax.numpy as jnp
from jax import lax
from jax.experimental import pallas as pl
from jax.experimental.pallas import tpu as pltpu
from jax.sharding import PartitionSpec as P

MESH = pl.DeviceIdType.MESH
BF = jnp.bfloat16
F32 = jnp.float32
CH = 4
ORDER = (
    ("p", 0), ("o", 0), ("o", 1), ("p", 1), ("p", 2), ("b", 0), ("o", 2), ("b", 1),
    ("o", 3), ("p", 3), ("v", 0), ("c", 0), ("b", 2), ("d", 0), ("c", 1), ("e", 0),
    ("b", 3), ("d", 1), ("m", 0), ("f", 0), ("g", 0), ("h", 0), ("c", 2), ("i", 0),
    ("e", 1), ("d", 2), ("m", 1), ("k", 0), ("f", 1), ("j", 0), ("g", 1), ("c", 3),
    ("h", 1), ("i", 1), ("d", 3), ("e", 2), ("m", 2), ("f", 2), ("g", 2), ("h", 2),
    ("k", 1), ("j", 1), ("e", 3), ("i", 2), ("m", 3), ("f", 3), ("g", 3), ("h", 3),
    ("k", 2), ("j", 2), ("i", 3), ("k", 3), ("j", 3), ("l", 0), ("l", 1), ("l", 2),
    ("l", 3),
)
NN = (((1,), (0,)), ((), ()))


def split(v):
    hi = v.astype(BF)
    return hi, (v - hi.astype(F32)).astype(BF)


def dot3(a, b, dims=NN):
    dot = lambda p, q: lax.dot_general(p, q, dims, preferred_element_type=F32)
    return dot(a[0], b[0]) + (dot(a[0], b[1]) + dot(a[1], b[0]))


def kernel(
    s_ref, panel_ref, linv_ref, mask_ref, sj_ref, jj_ref,
    so, sp, scat, uto, uts, utp, ucat, gu, bs,
    tt, ol, nl, yl, zl_, yts, yf, gs, gx, gz, gzl,
    s_loc, s_s, s_r, u_s, u_r, o_s, o_r, n_s, n_r, y_s, y_r, z_s, z_r,
    a_s, a_r, b_s, b_r, gx_s, gx_r, gz_s, gz_r, ga_s, ga_r, gb_s, gb_r, gc_s, gc_r, gd_s, gd_r,
):
    row = lax.axis_index("row")
    col = lax.axis_index("col")
    x, zh, k = row // 8, (row // 2) % 4, row % 2
    y, zl = col // 2, col % 2
    z = zh * 2 + zl
    other = 1 - k

    def dev(x, y, zh, zl, k):
        return ((x * 4 + zh) * 2 + k, y * 2 + zl)

    def at_x(d):
        return dev((x + d) % 4, y, zh, zl, k)

    def at_y(d):
        return dev(x, (y + d) % 4, zh, zl, k)

    def at_zh(d):
        return dev(x, y, (zh + d) % 4, zl, k)

    def at_z(d):
        t = (z + d) % 8
        return dev(x, y, t // 2, t % 2, k)

    partner = dev(x, y, zh, zl, other)
    cross = dev(x, y, zh, 1 - zl, other)
    peers = [partner, cross]
    peers += [at_x(d) for d in (1, 2, 3)] + [at_y(d) for d in (1, 2, 3)] + [at_z(d) for d in range(1, 8)]

    sent = []

    def remote(src, dst, send, recv, device):
        return pltpu.make_async_remote_copy(
            src_ref=src, dst_ref=dst, send_sem=send, recv_sem=recv, device_id=device, device_id_type=MESH
        )

    def push(src, dst, send, recv, device):
        copy = remote(src, dst, send, recv, device)
        copy.start()
        sent.append(copy)

    def arrived(dst, send, recv):
        remote(dst, dst, send, recv, partner).wait_recv()

    barrier = pltpu.get_barrier_semaphore()
    for peer in peers:
        pl.semaphore_signal(barrier, inc=1, device_id=peer, device_id_type=MESH)

    offs = (2, 1, 3, 0)
    local = []
    for p in range(4):
        copy = pltpu.make_async_copy(s_ref.at[:, :, (x + offs[p]) % 4], so.at[p], s_loc.at[p])
        copy.start()
        local.append(copy)

    def update(j):
        a = split(panel_ref[j])
        b = split(linv_ref[j])
        return dot3(a, b).T * mask_ref[j, 0:1, :]

    uts[...] = update(other)
    pl.semaphore_wait(barrier, len(peers))
    push(uts, utp, u_s.at[0], u_r.at[0], partner)
    for p in range(4):
        push(s_ref.at[:, :, (x + offs[p]) % 4], sp.at[p], s_s.at[p], s_r.at[p], partner)
    ut = update(k)
    uto[...] = ut
    ucat[:, 0:512], ucat[:, 1024:1536] = split(ut)

    def spread(p, half, src):
        def body(i, carry):
            r = pl.multiple_of(half * 512 + i * 128, 128)
            for m in range(4):
                hi, lo = split(src[p, i, m])
                scat[p, pl.ds(r, 128), m * 128 : (m + 1) * 128] = lo
                scat[p, pl.ds(1024 + r, 128), m * 128 : (m + 1) * 128] = hi
            return carry

        lax.fori_loop(0, 4, body, 0)

    def phase_p(p):
        local[p].wait()
        spread(p, 0, so)
        if p == 0:
            arrived(utp, u_s.at[0], u_r.at[0])
            ucat[:, 512:1024], ucat[:, 1536:2048] = split(utp[...])
        arrived(sp.at[p], s_s.at[p], s_r.at[p])
        spread(p, 1, sp)
        dot = lambda a, b: jnp.dot(a, b, preferred_element_type=F32)
        tt[p] = dot(ucat[...], scat[p]) + dot(ucat[:, 0:1024], scat[p, 1024:2048])

    def phase_o(t):
        r = t * 128
        push(tt.at[0, r : r + 64], ol.at[t, 0], o_s.at[t, 0], o_r.at[t, 0], at_x(1))
        push(tt.at[0, r + 64 : r + 128], ol.at[t, 1], o_s.at[t, 1], o_r.at[t, 1], at_x(3))

    def phase_v(t):
        @pl.when(k == zl)
        def _():
            gu[0], gu[1] = split(uto[...].T)

        @pl.when(k != zl)
        def _():
            gu[0], gu[1] = split(utp[...].T)

        uto[...] = linv_ref[k].T
        first = jnp.where((x == 0) & (z == 0), 1.0, 0.0).astype(F32)
        rows = [uto[pl.ds(pl.multiple_of(t * 128 + y * 32, 32), 32)] for t in range(CH)]
        base = dot3(split(jnp.concatenate(rows)), split(linv_ref[k])) * first
        for t in range(CH):
            bs[t] = base[t * 32 : t * 32 + 32]

    def phase_b(t):
        for s in (0, 1):
            arrived(ol.at[t, s], o_s.at[t, s], o_r.at[t, s])
            r = slice(t * 128 + s * 64, t * 128 + s * 64 + 64)
            tt[1 + s, r] = tt[1 + s, r] + ol[t, s]
            push(tt.at[1 + s, t * 128 : t * 128 + 128], nl.at[t, s], n_s.at[t, s], n_r.at[t, s], at_x(1 + 2 * s))

    def phase_c(t):
        for s in (0, 1):
            arrived(nl.at[t, s], n_s.at[t, s], n_r.at[t, s])
        r = slice(t * 128, t * 128 + 128)
        tt[3, r] = tt[3, r] + (nl[t, 0] + nl[t, 1])
        for d in (1, 2, 3):
            q = (y + d) % 4
            push(tt.at[3, pl.ds(pl.multiple_of(t * 128 + q * 32, 32), 32)], yl.at[t, y], y_s.at[t, d], y_r.at[t, y], at_y(d))
        yl[t, y] = tt[3, pl.ds(pl.multiple_of(t * 128 + y * 32, 32), 32)]

    def phase_d(t):
        for d in (1, 2, 3):
            q = (y + d) % 4
            arrived(yl.at[t, q], y_s.at[t, d], y_r.at[t, q])
        for d in (1, 2, 3):
            q = (zh + d) % 4
            push(yl.at[t, q], zl_.at[t, zh], z_s.at[t, d], z_r.at[t, zh], at_zh(d))

    def phase_e(t):
        yt = yl[t, zh]
        for d in (1, 2, 3):
            q = (zh + d) % 4
            arrived(zl_.at[t, q], z_s.at[t, d], z_r.at[t, q])
            yt = yt + zl_[t, q]
        yts[t] = yt

        @pl.when(k == zl)
        def _():
            yf[t, y, k] = yt

        @pl.when(k != zl)
        def _():
            remote(yts.at[t], yf.at[t, y, k], a_s.at[t, 0], a_r.at[t, k], partner).start()

        push(yts.at[t], yf.at[t, y, k], a_s.at[t, 1], a_r.at[t, k], dev(x, y, zh, 1 - zl, zl))
        yh, yl_ = split(yt)
        g = jnp.dot(jnp.concatenate([yh, yl_]), gu[0], preferred_element_type=F32)
        g2 = jnp.dot(yh, gu[1], preferred_element_type=F32)
        gs[t] = (g[0:32] + bs[t]) + (g[32:64] + g2)
        for d in (1, 2, 3):
            q = (x + d) % 4
            push(gs.at[t, pl.ds(pl.multiple_of(q * 8, 8), 8)], gx.at[t, x], gx_s.at[t, d], gx_r.at[t, x], at_x(d))

    def phase_f(t):
        arrived(yf.at[t, y, other], a_s.at[t, 0], a_r.at[t, other])

        @pl.when(k != zl)
        def _():
            arrived(yf.at[t, y, k], a_s.at[t, 0], a_r.at[t, k])

        for d in (1, 2, 3):
            push(yf.at[t, y], yf.at[t, y], b_s.at[t, d], b_r.at[t, y], at_y(d))
    def phase_m(t):
        g = gs[t, pl.ds(pl.multiple_of(x * 8, 8), 8)]
        for d in (1, 2, 3):
            q = (x + d) % 4
            arrived(gx.at[t, q], gx_s.at[t, d], gx_r.at[t, q])
            g = g + gx[t, q]
        for q in range(4):
            gz[t, q] = g[:, q * 128 : (q + 1) * 128]
        for d in range(1, 8):
            q = (z + d) % 8
            push(gz.at[t, q // 2], gzl.at[t, z], gz_s.at[t, d], gz_r.at[t, z], at_z(d))

    def tile_row(t, x, y):
        return pl.multiple_of(t * 128 + y * 32 + x * 8, 8)

    def phase_g(t):
        g = gz[t, zh]
        for d in range(1, 8):
            q = (z + d) % 8
            arrived(gzl.at[t, q], gz_s.at[t, d], gz_r.at[t, q])
            g = g + gzl[t, q]
        r = pl.ds(tile_row(t, x, y), 8)
        c = pl.ds(pl.multiple_of(zh * 128, 128), 128)
        jj_ref[k, r, c] = g
        for d in (1, 2, 3):
            push(jj_ref.at[k, r, c], jj_ref.at[k, r, c], ga_s.at[t, d], ga_r.at[t, zh], at_zh(d))

    def phase_h(t):
        r = pl.ds(tile_row(t, x, y), 8)
        for d in (1, 2, 3):
            q = (zh + d) % 4
            c = pl.ds(pl.multiple_of(q * 128, 128), 128)
            arrived(jj_ref.at[k, r, c], ga_s.at[t, d], ga_r.at[t, q])
        for d in (1, 2, 3):
            push(jj_ref.at[k, r], jj_ref.at[k, r], gb_s.at[t, d], gb_r.at[t, x], at_x(d))

    def phase_i(t):
        for d in (1, 2, 3):
            q = (x + d) % 4
            arrived(jj_ref.at[k, pl.ds(tile_row(t, q, y), 8)], gb_s.at[t, d], gb_r.at[t, q])
        r = pl.ds(pl.multiple_of(t * 128 + y * 32, 32), 32)
        for d in (1, 2, 3):
            push(jj_ref.at[k, r], jj_ref.at[k, r], gc_s.at[t, d], gc_r.at[t, y], at_y(d))

    def phase_j(t):
        for d in (1, 2, 3):
            q = (y + d) % 4
            arrived(jj_ref.at[k, pl.ds(pl.multiple_of(t * 128 + q * 32, 32), 32)], gc_s.at[t, d], gc_r.at[t, q])
        r = slice(t * 128, t * 128 + 128)
        push(jj_ref.at[k, r], jj_ref.at[k, r], gd_s.at[t], gd_r.at[t], partner)

    def phase_k(t):
        for d in (1, 2, 3):
            q = (y + d) % 4
            arrived(yf.at[t, q], b_s.at[t, d], b_r.at[t, q])
        for j in range(2):
            v = yf[t, :, j].reshape(128, 512) * (-mask_ref[j, 0:1, :])
            v = v.T
            for i in range(4):
                sj_ref[j, i, :, t * 128 : (t + 1) * 128] = v[i * 128 : (i + 1) * 128]

    def phase_l(t):
        arrived(jj_ref.at[other, t * 128 : t * 128 + 128], gd_s.at[t], gd_r.at[t])

    phases = dict(
        o=phase_o, p=phase_p, v=phase_v, b=phase_b, c=phase_c, d=phase_d, e=phase_e, f=phase_f, g=phase_g,
        h=phase_h, i=phase_i, j=phase_j, k=phase_k, l=phase_l, m=phase_m,
    )
    for name, t in ORDER:
        phases[name](t)

    for copy in sent:
        copy.wait_send()

    @pl.when(k != zl)
    def _():
        for t in range(CH):
            remote(yts.at[t], yf.at[t, y, k], a_s.at[t, 0], a_r.at[t, k], partner).wait_send()


def local(sigma_anc, panel, pattern, linv):
    row_ids = jnp.arange(4, dtype=jnp.int32) * 32 + lax.axis_index("row")
    in_pattern = jnp.any(pattern[:, :, None] == row_ids[None, None, :], axis=1).astype(F32)
    mask = jnp.broadcast_to(in_pattern[:, None, :, None], (2, 8, 4, 128)).reshape(2, 8, 512)
    s = sigma_anc.reshape(4, 4, 4, 128, 128)
    dma = pltpu.SemaphoreType.DMA
    vm = lambda *shape: pltpu.VMEM(shape, F32)
    vb = lambda *shape: pltpu.VMEM(shape, BF)
    pair = lambda *shape: [dma(shape), dma(shape)]
    return pl.pallas_call(
        kernel,
        out_shape=(
            jax.ShapeDtypeStruct((2, 4, 128, 512), F32),
            jax.ShapeDtypeStruct((2, 512, 512), F32),
        ),
        in_specs=[pl.BlockSpec(memory_space=pl.ANY)] + [pl.BlockSpec(memory_space=pltpu.VMEM)] * 3,
        out_specs=[pl.BlockSpec(memory_space=pltpu.VMEM)] * 2,
        scratch_shapes=[
            vm(4, 4, 4, 128, 128), vm(4, 4, 4, 128, 128),
            vb(4, 2048, 512), vm(512, 512), vm(512, 512), vm(512, 512), vb(512, 2048), vb(2, 512, 512),
            vm(CH, 32, 512), vm(4, 512, 512), vm(CH, 2, 64, 512), vm(CH, 2, 128, 512),
            vm(CH, 4, 32, 512), vm(CH, 4, 32, 512), vm(CH, 32, 512), vm(CH, 4, 2, 32, 512),
            vm(CH, 32, 512), vm(CH, 4, 8, 512), vm(CH, 4, 8, 128), vm(CH, 8, 8, 128),
            dma((4,)), *pair(4), *pair(1), *pair(CH, 2), *pair(CH, 2), *pair(CH, 4), *pair(CH, 4),
            *pair(CH, 2), *pair(CH, 4), *pair(CH, 4), *pair(CH, 8), *pair(CH, 4), *pair(CH, 4), *pair(CH, 4), *pair(CH),
        ],
        compiler_params=pltpu.CompilerParams(
            collective_id=0, has_side_effects=True, vmem_limit_bytes=60 << 20
        ),
        name="selinv",
    )(s, panel.reshape(2, 512, 512), linv, mask)


def solution(mesh):
    return jax.shard_map(
        local,
        mesh=mesh,
        in_specs=(P("row", "col", None, None), P(None, "row", None, None), P(), P()),
        out_specs=(P(None, "row", None, None), P()),
        check_vma=False,
    )
```

time: 794 us -> 133 us (0.17)
  waiting for transfers between devices: 721 us -> 0 us
  Pallas kernels: 0 us -> 126 us
  matrix products: 42.1 us -> 0 us
  between operations: 13.8 us -> 0.66 us
    psum x3 -> x0, waiting for transfers between devices: 721 us -> none  [the longest x1 328 us: local(): gathered_cols = lax.psum(local_cols, 'row')]
    pallas_call x0 -> x1, Pallas kernels: none -> 126 us  [local(): pl.pallas_call(kernel, out_shape=(jax.ShapeDtypeStruct((2, 4, 128, 512),...]
    dot_general x5 -> x0, matrix products: 42.1 us -> none  [the longest x1 17.7 us: local(): jnp.einsum('qkij,skjw->sqiw', sigma_anc, gathered_cols, precision=highest...]
    dot_general x1 -> x0, local copies, waits for them, and re-layouts: 10 us -> none  [local(): jnp.einsum('kq,sqiw->skiw', selector, updated, precision=highest, preferr...]
  transfers between devices with their start and end apart: 3 -> 0, of which waited for: 3 -> 0; matrix products, arithmetic and copies ran while one was open for 0% -> 0% of each run, Pallas kernels for 0% -> 0%
where the time goes in v1:
time: 133 us
  Pallas kernels  126 us (95%)
  local copies, waits for them, and re-layouts  5.25 us (4%)
    pallas_call x1, Pallas kernels, local(): pl.pallas_call(kernel, out_shape=(jax.ShapeDtypeStruct((2, 4, 128, 512),...  126 us
    unnamed x6, local copies, waits for them, and re-layouts  4.63 us

profile of v1, /device:TPU:1, one launch (start us, length us, event | category | flops | bytes accessed | tf_op | source)
XLA Modules:
  0.0 132.7 jit_solution(14776810317215619467)
XLA Ops:
  0.6 0.9 compare_reduce_fusion
  1.5 0.1 broadcast_bitcast_fusion
  1.6 0.6 broadcast_in_dim.14.mask_ref
  2.2 125.9 %selinv.1 = (f32[2,4,128,512]{3,2,1,0:T(8,128)}, f32[2,512,512]{2,1,0:T(8,128)}) custom-call(f32[4,4,4,128,128]{4,3,2,1,0:T(8,128)} %bitcast.7, f32[2,512,512]{2,1,0:T(8,128)} %bitcast.8, f32[2,512,512]{2,1,0:T(8,128)} %linv_ref.1, f32[2,8,512]{2,1,0:T(8,128)} %broadcast_in_dim.14.mask_ref), custom_call_target="tpu_custom_call" | custom-call | tf_op jit(solution)/shard_map/selinv/pallas_call | solution.py:301
  128.1 0.0 copy-start
  128.1 3.2 %copy.11 = f32[2,4,128,512]{3,2,1,0:T(8,128)} copy(f32[2,4,128,512]{3,2,1,0:T(8,128)} %get-tuple-element.4) | data formatting | bytes 4194304
  131.3 0.0 copy-done
  131.3 1.3 copy.12
  (3 shorter events, 0.0 us)
Async XLA Ops:
  128.1 3.2 %copy-start = (f32[2,512,512]{2,1,0:T(8,128)S(1)}, f32[2,512,512]{2,1,0:T(8,128)}, u32[]{:S(2)}) copy-start(f32[2,512,512]{2,1,0:T(8,128)} %get-tuple-element.5) | copy-start | bytes 6291460

commit v2 on v1

--- a/solution.py
+++ b/solution.py
@@ -11,12 +11,11 @@
 CH = 4
 ORDER = (
     ("p", 0), ("o", 0), ("o", 1), ("p", 1), ("p", 2), ("b", 0), ("o", 2), ("b", 1),
-    ("o", 3), ("p", 3), ("v", 0), ("c", 0), ("b", 2), ("d", 0), ("c", 1), ("e", 0),
-    ("b", 3), ("d", 1), ("m", 0), ("f", 0), ("g", 0), ("h", 0), ("c", 2), ("i", 0),
-    ("e", 1), ("d", 2), ("m", 1), ("k", 0), ("f", 1), ("j", 0), ("g", 1), ("c", 3),
-    ("h", 1), ("i", 1), ("d", 3), ("e", 2), ("m", 2), ("f", 2), ("g", 2), ("h", 2),
-    ("k", 1), ("j", 1), ("e", 3), ("i", 2), ("m", 3), ("f", 3), ("g", 3), ("h", 3),
-    ("k", 2), ("j", 2), ("i", 3), ("k", 3), ("j", 3), ("l", 0), ("l", 1), ("l", 2),
+    ("o", 3), ("p", 3), ("v", 0), ("c", 0), ("b", 2), ("d", 0), ("b", 3), ("c", 1),
+    ("d", 1), ("e", 0), ("c", 2), ("d", 2), ("m", 0), ("e", 1), ("f", 0), ("c", 3),
+    ("d", 3), ("m", 1), ("e", 2), ("k", 0), ("g", 0), ("m", 2), ("f", 1), ("g", 1),
+    ("h", 0), ("l", 0), ("e", 3), ("f", 2), ("m", 3), ("k", 1), ("g", 2), ("h", 1),
+    ("l", 1), ("f", 3), ("g", 3), ("k", 2), ("h", 2), ("l", 2), ("h", 3), ("k", 3),
     ("l", 3),
 )
 NN = (((1,), (0,)), ((), ()))
@@ -34,10 +33,10 @@
 
 def kernel(
     s_ref, panel_ref, linv_ref, mask_ref, sj_ref, jj_ref,
-    so, sp, scat, uto, uts, utp, ucat, gu, bs,
-    tt, ol, nl, yl, zl_, yts, yf, gs, gx, gz, gzl,
-    s_loc, s_s, s_r, u_s, u_r, o_s, o_r, n_s, n_r, y_s, y_r, z_s, z_r,
-    a_s, a_r, b_s, b_r, gx_s, gx_r, gz_s, gz_r, ga_s, ga_r, gb_s, gb_r, gc_s, gc_r, gd_s, gd_r,
+    pbuf, lbuf, sjv, jjv, so, sp, scat, uto, uts, utp, ucat, gu, bs,
+    tt, ol, nl, yl, zl_, yts, yf, gs, gx, gzl,
+    in_s, out_s, s_loc, s_s, s_r, u_s, u_r, o_s, o_r, n_s, n_r, y_s, y_r, z_s, z_r,
+    a_s, a_r, b_s, b_r, gx_s, gx_r, gz_s, gz_r, gb_s, gb_r, gd_s, gd_r,
 ):
     row = lax.axis_index("row")
     col = lax.axis_index("col")
@@ -65,9 +64,10 @@
     partner = dev(x, y, zh, zl, other)
     cross = dev(x, y, zh, 1 - zl, other)
     peers = [partner, cross]
-    peers += [at_x(d) for d in (1, 2, 3)] + [at_y(d) for d in (1, 2, 3)] + [at_z(d) for d in range(1, 8)]
-
-    sent = []
+    peers += [at_z(d) for d in range(1, 8)]
+    peers += [dev((x + n // 4) % 4, (y + n % 4) % 4, zh, zl, k) for n in range(1, 16)]
+
+    sent, outs = [], []
 
     def remote(src, dst, send, recv, device):
         return pltpu.make_async_remote_copy(
@@ -85,6 +85,13 @@
     barrier = pltpu.get_barrier_semaphore()
     for peer in peers:
         pl.semaphore_signal(barrier, inc=1, device_id=peer, device_id_type=MESH)
+
+    loads = []
+    for n, j in enumerate((other, k)):
+        for m, (src, dst) in enumerate(((panel_ref, pbuf), (linv_ref, lbuf))):
+            copy = pltpu.make_async_copy(src.at[j], dst.at[j], in_s.at[n, m])
+            copy.start()
+            loads.append(copy)
 
     offs = (2, 1, 3, 0)
     local = []
@@ -94,15 +101,21 @@
         local.append(copy)
 
     def update(j):
-        a = split(panel_ref[j])
-        b = split(linv_ref[j])
+        a = split(pbuf[j])
+        b = split(lbuf[j])
         return dot3(a, b).T * mask_ref[j, 0:1, :]
 
+    loads[0].wait()
+    loads[1].wait()
     uts[...] = update(other)
     pl.semaphore_wait(barrier, len(peers))
-    push(uts, utp, u_s.at[0], u_r.at[0], partner)
     for p in range(4):
-        push(s_ref.at[:, :, (x + offs[p]) % 4], sp.at[p], s_s.at[p], s_r.at[p], partner)
+        local[p].wait()
+        push(so.at[p], sp.at[p], s_s.at[p], s_r.at[p], partner)
+        if p == 0:
+            push(uts, utp, u_s.at[0], u_r.at[0], partner)
+    loads[2].wait()
+    loads[3].wait()
     ut = update(k)
     uto[...] = ut
     ucat[:, 0:512], ucat[:, 1024:1536] = split(ut)
@@ -119,7 +132,6 @@
         lax.fori_loop(0, 4, body, 0)
 
     def phase_p(p):
-        local[p].wait()
         spread(p, 0, so)
         if p == 0:
             arrived(utp, u_s.at[0], u_r.at[0])
@@ -143,10 +155,10 @@
         def _():
             gu[0], gu[1] = split(utp[...].T)
 
-        uto[...] = linv_ref[k].T
+        uto[...] = lbuf[k].T
         first = jnp.where((x == 0) & (z == 0), 1.0, 0.0).astype(F32)
         rows = [uto[pl.ds(pl.multiple_of(t * 128 + y * 32, 32), 32)] for t in range(CH)]
-        base = dot3(split(jnp.concatenate(rows)), split(linv_ref[k])) * first
+        base = dot3(split(jnp.concatenate(rows)), split(lbuf[k])) * first
         for t in range(CH):
             bs[t] = base[t * 32 : t * 32 + 32]
 
@@ -193,12 +205,13 @@
 
         push(yts.at[t], yf.at[t, y, k], a_s.at[t, 1], a_r.at[t, k], dev(x, y, zh, 1 - zl, zl))
         yh, yl_ = split(yt)
-        g = jnp.dot(jnp.concatenate([yh, yl_]), gu[0], preferred_element_type=F32)
-        g2 = jnp.dot(yh, gu[1], preferred_element_type=F32)
-        gs[t] = (g[0:32] + bs[t]) + (g[32:64] + g2)
-        for d in (1, 2, 3):
-            q = (x + d) % 4
-            push(gs.at[t, pl.ds(pl.multiple_of(q * 8, 8), 8)], gx.at[t, x], gx_s.at[t, d], gx_r.at[t, x], at_x(d))
+        c = slice(t * 128, 512)
+        g = jnp.dot(jnp.concatenate([yh, yl_]), gu[0, :, c], preferred_element_type=F32)
+        g2 = jnp.dot(yh, gu[1, :, c], preferred_element_type=F32)
+        gs[t, :, c] = (g[0:32] + bs[t, :, c]) + (g[32:64] + g2)
+        for d in (1, 2, 3):
+            r = pl.ds(pl.multiple_of((x + d) % 4 * 8, 8), 8)
+            push(gs.at[t, r, c], gx.at[t, x, :, c], gx_s.at[t, d], gx_r.at[t, x], at_x(d))
 
     def phase_f(t):
         arrived(yf.at[t, y, other], a_s.at[t, 0], a_r.at[t, other])
@@ -210,55 +223,57 @@
         for d in (1, 2, 3):
             push(yf.at[t, y], yf.at[t, y], b_s.at[t, d], b_r.at[t, y], at_y(d))
     def phase_m(t):
-        g = gs[t, pl.ds(pl.multiple_of(x * 8, 8), 8)]
+        c = slice(t * 128, 512)
+        g = gs[t, pl.ds(pl.multiple_of(x * 8, 8), 8), c]
         for d in (1, 2, 3):
             q = (x + d) % 4
-            arrived(gx.at[t, q], gx_s.at[t, d], gx_r.at[t, q])
-            g = g + gx[t, q]
-        for q in range(4):
-            gz[t, q] = g[:, q * 128 : (q + 1) * 128]
+            arrived(gx.at[t, q, :, c], gx_s.at[t, d], gx_r.at[t, q])
+            g = g + gx[t, q, :, c]
+        gzl[t, z, :, c] = g
+        for d in range(1, 8):
+            push(gzl.at[t, z, :, c], gzl.at[t, z, :, c], gz_s.at[t, d], gz_r.at[t, z], at_z(d))
+
+    def tile_row(t, x, y):
+        return pl.ds(pl.multiple_of(t * 128 + y * 32 + x * 8, 8), 8)
+
+    def phase_g(t):
+        c = slice(t * 128, 512)
         for d in range(1, 8):
             q = (z + d) % 8
-            push(gz.at[t, q // 2], gzl.at[t, z], gz_s.at[t, d], gz_r.at[t, z], at_z(d))
-
-    def tile_row(t, x, y):
-        return pl.multiple_of(t * 128 + y * 32 + x * 8, 8)
-
-    def phase_g(t):
-        g = gz[t, zh]
-        for d in range(1, 8):
-            q = (z + d) % 8
-            arrived(gzl.at[t, q], gz_s.at[t, d], gz_r.at[t, q])
-            g = g + gzl[t, q]
-        r = pl.ds(tile_row(t, x, y), 8)
-        c = pl.ds(pl.multiple_of(zh * 128, 128), 128)
-        jj_ref[k, r, c] = g
-        for d in (1, 2, 3):
-            push(jj_ref.at[k, r, c], jj_ref.at[k, r, c], ga_s.at[t, d], ga_r.at[t, zh], at_zh(d))
+            arrived(gzl.at[t, q, :, c], gz_s.at[t, d], gz_r.at[t, q])
+        g = gzl[t, 0, :, c]
+        for q in range(1, 8):
+            g = g + gzl[t, q, :, c]
+        r = tile_row(t, x, y)
+        jjv[k, r, c] = g
+        for n in range(1, 16):
+            dx, dy = n // 4, n % 4
+            push(
+                jjv.at[k, r, c], jjv.at[k, r, c], gb_s.at[t, n], gb_r.at[t, x * 4 + y],
+                dev((x + dx) % 4, (y + dy) % 4, zh, zl, k),
+            )
+
+    def store(t, j, side):
+        r, c = slice(t * 128, t * 128 + 128), slice(t * 128, 512)
+        if side:
+            r, c = slice(t * 128 + 128, 512), r
+        copy = pltpu.make_async_copy(jjv.at[j, r, c], jj_ref.at[j, r, c], out_s.at[t, side, j])
+        copy.start()
+        outs.append(copy)
+
+    def mirror(t, j):
+        r = slice(t * 128, t * 128 + 128)
+        for n in range(t + 1, 4):
+            c = slice(n * 128, n * 128 + 128)
+            jjv[j, c, r] = jjv[j, r, c].T
 
     def phase_h(t):
-        r = pl.ds(tile_row(t, x, y), 8)
-        for d in (1, 2, 3):
-            q = (zh + d) % 4
-            c = pl.ds(pl.multiple_of(q * 128, 128), 128)
-            arrived(jj_ref.at[k, r, c], ga_s.at[t, d], ga_r.at[t, q])
-        for d in (1, 2, 3):
-            push(jj_ref.at[k, r], jj_ref.at[k, r], gb_s.at[t, d], gb_r.at[t, x], at_x(d))
-
-    def phase_i(t):
-        for d in (1, 2, 3):
-            q = (x + d) % 4
-            arrived(jj_ref.at[k, pl.ds(tile_row(t, q, y), 8)], gb_s.at[t, d], gb_r.at[t, q])
-        r = pl.ds(pl.multiple_of(t * 128 + y * 32, 32), 32)
-        for d in (1, 2, 3):
-            push(jj_ref.at[k, r], jj_ref.at[k, r], gc_s.at[t, d], gc_r.at[t, y], at_y(d))
-
-    def phase_j(t):
-        for d in (1, 2, 3):
-            q = (y + d) % 4
-            arrived(jj_ref.at[k, pl.ds(pl.multiple_of(t * 128 + q * 32, 32), 32)], gc_s.at[t, d], gc_r.at[t, q])
-        r = slice(t * 128, t * 128 + 128)
-        push(jj_ref.at[k, r], jj_ref.at[k, r], gd_s.at[t], gd_r.at[t], partner)
+        r, c = slice(t * 128, t * 128 + 128), slice(t * 128, 512)
+        for n in range(1, 16):
+            dx, dy = n // 4, n % 4
+            qx, qy = (x + dx) % 4, (y + dy) % 4
+            arrived(jjv.at[k, tile_row(t, qx, qy), c], gb_s.at[t, n], gb_r.at[t, qx * 4 + qy])
+        push(jjv.at[k, r, c], jjv.at[k, r, c], gd_s.at[t], gd_r.at[t], partner)
 
     def phase_k(t):
         for d in (1, 2, 3):
@@ -268,20 +283,32 @@
             v = yf[t, :, j].reshape(128, 512) * (-mask_ref[j, 0:1, :])
             v = v.T
             for i in range(4):
-                sj_ref[j, i, :, t * 128 : (t + 1) * 128] = v[i * 128 : (i + 1) * 128]
+                sjv[j, i, :, t * 128 : (t + 1) * 128] = v[i * 128 : (i + 1) * 128]
+        c = slice(t * 128, t * 128 + 128)
+        copy = pltpu.make_async_copy(sjv.at[:, :, :, c], sj_ref.at[:, :, :, c], out_s.at[t, 2, 0])
+        copy.start()
+        outs.append(copy)
 
     def phase_l(t):
-        arrived(jj_ref.at[other, t * 128 : t * 128 + 128], gd_s.at[t], gd_r.at[t])
+        r, c = slice(t * 128, t * 128 + 128), slice(t * 128, 512)
+        arrived(jjv.at[other, r, c], gd_s.at[t], gd_r.at[t])
+        for j in range(2):
+            store(t, j, 0)
+            if t < 3:
+                mirror(t, j)
+                store(t, j, 1)
 
     phases = dict(
         o=phase_o, p=phase_p, v=phase_v, b=phase_b, c=phase_c, d=phase_d, e=phase_e, f=phase_f, g=phase_g,
-        h=phase_h, i=phase_i, j=phase_j, k=phase_k, l=phase_l, m=phase_m,
+        h=phase_h, k=phase_k, l=phase_l, m=phase_m,
     )
     for name, t in ORDER:
         phases[name](t)
 
     for copy in sent:
         copy.wait_send()
+    for copy in outs:
+        copy.wait()
 
     @pl.when(k != zl)
     def _():
@@ -304,16 +331,17 @@
             jax.ShapeDtypeStruct((2, 4, 128, 512), F32),
             jax.ShapeDtypeStruct((2, 512, 512), F32),
         ),
-        in_specs=[pl.BlockSpec(memory_space=pl.ANY)] + [pl.BlockSpec(memory_space=pltpu.VMEM)] * 3,
-        out_specs=[pl.BlockSpec(memory_space=pltpu.VMEM)] * 2,
+        in_specs=[pl.BlockSpec(memory_space=pl.ANY)] * 3 + [pl.BlockSpec(memory_space=pltpu.VMEM)],
+        out_specs=[pl.BlockSpec(memory_space=pl.ANY)] * 2,
         scratch_shapes=[
+            vm(2, 512, 512), vm(2, 512, 512), vm(2, 4, 128, 512), vm(2, 512, 512),
             vm(4, 4, 4, 128, 128), vm(4, 4, 4, 128, 128),
             vb(4, 2048, 512), vm(512, 512), vm(512, 512), vm(512, 512), vb(512, 2048), vb(2, 512, 512),
             vm(CH, 32, 512), vm(4, 512, 512), vm(CH, 2, 64, 512), vm(CH, 2, 128, 512),
             vm(CH, 4, 32, 512), vm(CH, 4, 32, 512), vm(CH, 32, 512), vm(CH, 4, 2, 32, 512),
-            vm(CH, 32, 512), vm(CH, 4, 8, 512), vm(CH, 4, 8, 128), vm(CH, 8, 8, 128),
-            dma((4,)), *pair(4), *pair(1), *pair(CH, 2), *pair(CH, 2), *pair(CH, 4), *pair(CH, 4),
-            *pair(CH, 2), *pair(CH, 4), *pair(CH, 4), *pair(CH, 8), *pair(CH, 4), *pair(CH, 4), *pair(CH, 4), *pair(CH),
+            vm(CH, 32, 512), vm(CH, 4, 8, 512), vm(CH, 8, 8, 512),
+            dma((2, 2)), dma((CH, 3, 2)), dma((4,)), *pair(4), *pair(1), *pair(CH, 2), *pair(CH, 2), *pair(CH, 4), *pair(CH, 4),
+            *pair(CH, 2), *pair(CH, 4), *pair(CH, 4), *pair(CH, 8), *pair(CH, 16), *pair(CH),
         ],
         compiler_params=pltpu.CompilerParams(
             collective_id=0, has_side_effects=True, vmem_limit_bytes=60 << 20

time: 133 us -> 109 us (0.82)
  Pallas kernels: 126 us -> 102 us
    pallas_call x1, Pallas kernels: 126 us -> 102 us  [local(): pl.pallas_call(kernel, out_shape=(jax.ShapeDtypeStruct((2, 4, 128, 512),...]
where the time goes in v2:
time: 109 us
  Pallas kernels  102 us (94%)
  local copies, waits for them, and re-layouts  5.25 us (5%)
    pallas_call x1, Pallas kernels, local(): pl.pallas_call(kernel, out_shape=(jax.ShapeDtypeStruct((2, 4, 128, 512),...  102 us
    unnamed x6, local copies, waits for them, and re-layouts  4.63 us

profile of v2, /device:TPU:1, one launch (start us, length us, event | category | flops | bytes accessed | tf_op | source)
XLA Modules:
  0.0 109.3 jit_solution(1554123918524678617)
XLA Ops:
  0.6 0.9 compare_reduce_fusion
  1.5 0.1 broadcast_bitcast_fusion
  1.6 0.6 broadcast_in_dim.14.mask_ref
  2.2 102.5 %selinv.1 = (f32[2,4,128,512]{3,2,1,0:T(8,128)}, f32[2,512,512]{2,1,0:T(8,128)}) custom-call(f32[4,4,4,128,128]{4,3,2,1,0:T(8,128)} %bitcast.7, f32[2,512,512]{2,1,0:T(8,128)} %bitcast.8, f32[2,512,512]{2,1,0:T(8,128)} %linv_ref.1, f32[2,8,512]{2,1,0:T(8,128)} %broadcast_in_dim.14.mask_ref), custom_call_target="tpu_custom_call" | custom-call | tf_op jit(solution)/shard_map/selinv/pallas_call | solution.py:328
  104.7 0.0 copy-start
  104.7 3.2 %copy.11 = f32[2,4,128,512]{3,2,1,0:T(8,128)} copy(f32[2,4,128,512]{3,2,1,0:T(8,128)} %get-tuple-element.4) | data formatting | bytes 4194304
  107.9 0.0 copy-done
  107.9 1.3 %copy.12 = f32[2,512,512]{2,1,0:T(8,128)} copy(f32[2,512,512]{2,1,0:T(8,128)S(1)} %copy-done) | data formatting | bytes 4194304
  (3 shorter events, 0.0 us)
Async XLA Ops:
  104.7 3.2 %copy-start = (f32[2,512,512]{2,1,0:T(8,128)S(1)}, f32[2,512,512]{2,1,0:T(8,128)}, u32[]{:S(2)}) copy-start(f32[2,512,512]{2,1,0:T(8,128)} %get-tuple-element.5) | copy-start | bytes 6291460

commit v3 on v2

--- a/solution.py
+++ b/solution.py
@@ -10,13 +10,13 @@
 F32 = jnp.float32
 CH = 4
 ORDER = (
-    ("p", 0), ("o", 0), ("o", 1), ("p", 1), ("p", 2), ("b", 0), ("o", 2), ("b", 1),
-    ("o", 3), ("p", 3), ("v", 0), ("c", 0), ("b", 2), ("d", 0), ("b", 3), ("c", 1),
-    ("d", 1), ("e", 0), ("c", 2), ("d", 2), ("m", 0), ("e", 1), ("f", 0), ("c", 3),
-    ("d", 3), ("m", 1), ("e", 2), ("k", 0), ("g", 0), ("m", 2), ("f", 1), ("g", 1),
-    ("h", 0), ("l", 0), ("e", 3), ("f", 2), ("m", 3), ("k", 1), ("g", 2), ("h", 1),
-    ("l", 1), ("f", 3), ("g", 3), ("k", 2), ("h", 2), ("l", 2), ("h", 3), ("k", 3),
-    ("l", 3),
+    ("q", 0), ("o", 0), ("o", 1), ("q", 1), ("o", 2), ("p", 1), ("p", 2), ("b", 0),
+    ("o", 3), ("b", 1), ("p", 3), ("v", 0), ("c", 0), ("b", 2), ("d", 0), ("b", 3),
+    ("c", 1), ("d", 1), ("e", 0), ("c", 2), ("d", 2), ("m", 0), ("e", 1), ("f", 0),
+    ("c", 3), ("d", 3), ("m", 1), ("e", 2), ("f", 1), ("k", 0), ("g", 0), ("m", 2),
+    ("f", 2), ("e", 3), ("g", 1), ("m", 3), ("f", 3), ("h", 0), ("l", 0), ("g", 2),
+    ("g", 3), ("h", 1), ("l", 1), ("k", 1), ("h", 2), ("l", 2), ("h", 3), ("l", 3),
+    ("k", 2), ("k", 3),
 )
 NN = (((1,), (0,)), ((), ()))
 
@@ -32,8 +32,8 @@
 
 
 def kernel(
-    s_ref, panel_ref, linv_ref, mask_ref, sj_ref, jj_ref,
-    pbuf, lbuf, sjv, jjv, so, sp, scat, uto, uts, utp, ucat, gu, bs,
+    s_ref, panel_ref, linv_ref, pattern_ref, sj_ref, jj_ref,
+    mask_ref, pbuf, lbuf, sjv, jjv, so, sp, scat, uto, uts, utp, ucat, gu, bs,
     tt, ol, nl, yl, zl_, yts, yf, gs, gx, gzl,
     in_s, out_s, s_loc, s_s, s_r, u_s, u_r, o_s, o_r, n_s, n_r, y_s, y_r, z_s, z_r,
     a_s, a_r, b_s, b_r, gx_s, gx_r, gz_s, gz_r, gb_s, gb_r, gd_s, gd_r,
@@ -100,25 +100,51 @@
         copy.start()
         local.append(copy)
 
-    def update(j):
-        a = split(pbuf[j])
-        b = split(lbuf[j])
+    pattern = pattern_ref[...]
+    for i in range(4):
+        hit = jnp.where(pattern == i * 32 + row, 1.0, 0.0).astype(F32)
+        for j in range(2):
+            value = jnp.max(hit[j : j + 1], axis=1, keepdims=True)
+            mask_ref[j, :, i * 128 : (i + 1) * 128] = jnp.broadcast_to(value, (8, 128))
+
+    def update(j, a, h):
+        b = split(lbuf[j, h * 256 : 512, h * 256 : h * 256 + 256])
+        a = tuple(v[:, h * 256 :] for v in a)
         return dot3(a, b).T * mask_ref[j, 0:1, :]
+
+    def update_other(h):
+        r = slice(h * 256, h * 256 + 256)
+        uts[r] = update(other, panel_other, h)
+
+    def push_other(h):
+        r = slice(h * 256, h * 256 + 256)
+        push(uts.at[r], utp.at[r], u_s.at[h], u_r.at[h], partner)
+
+    def update_own(h):
+        r = slice(h * 256, h * 256 + 256)
+        ut = update(k, panel_own, h)
+        uto[r] = ut
+        ucat[r, 0:512], ucat[r, 1024:1536] = split(ut)
+
+    def receive(h):
+        r = slice(h * 256, h * 256 + 256)
+        arrived(utp.at[r], u_s.at[h], u_r.at[h])
+        ucat[r, 512:1024], ucat[r, 1536:2048] = split(utp[r])
 
     loads[0].wait()
     loads[1].wait()
-    uts[...] = update(other)
+    panel_other = split(pbuf[other])
+    update_other(0)
     pl.semaphore_wait(barrier, len(peers))
     for p in range(4):
         local[p].wait()
         push(so.at[p], sp.at[p], s_s.at[p], s_r.at[p], partner)
         if p == 0:
-            push(uts, utp, u_s.at[0], u_r.at[0], partner)
+            push_other(0)
     loads[2].wait()
     loads[3].wait()
-    ut = update(k)
-    uto[...] = ut
-    ucat[:, 0:512], ucat[:, 1024:1536] = split(ut)
+    panel_own = split(pbuf[k])
+    update_own(0)
 
     def spread(p, half, src):
         def body(i, carry):
@@ -131,15 +157,28 @@
 
         lax.fori_loop(0, 4, body, 0)
 
+    def multiply(p, r):
+        dot = lambda a, b: jnp.dot(a, b, preferred_element_type=F32)
+        tt[p, r] = dot(ucat[r], scat[p]) + dot(ucat[r, 0:1024], scat[p, 1024:2048])
+
+    def phase_q(h):
+        if h == 0:
+            spread(0, 0, so)
+        else:
+            update_other(1)
+            push_other(1)
+            update_own(1)
+        receive(h)
+        if h == 0:
+            arrived(sp.at[0], s_s.at[0], s_r.at[0])
+            spread(0, 1, sp)
+        multiply(0, slice(h * 256, h * 256 + 256))
+
     def phase_p(p):
         spread(p, 0, so)
-        if p == 0:
-            arrived(utp, u_s.at[0], u_r.at[0])
-            ucat[:, 512:1024], ucat[:, 1536:2048] = split(utp[...])
         arrived(sp.at[p], s_s.at[p], s_r.at[p])
         spread(p, 1, sp)
-        dot = lambda a, b: jnp.dot(a, b, preferred_element_type=F32)
-        tt[p] = dot(ucat[...], scat[p]) + dot(ucat[:, 0:1024], scat[p, 1024:2048])
+        multiply(p, slice(0, 512))
 
     def phase_o(t):
         r = t * 128
@@ -299,7 +338,7 @@
                 store(t, j, 1)
 
     phases = dict(
-        o=phase_o, p=phase_p, v=phase_v, b=phase_b, c=phase_c, d=phase_d, e=phase_e, f=phase_f, g=phase_g,
+        o=phase_o, p=phase_p, q=phase_q, v=phase_v, b=phase_b, c=phase_c, d=phase_d, e=phase_e, f=phase_f, g=phase_g,
         h=phase_h, k=phase_k, l=phase_l, m=phase_m,
     )
     for name, t in ORDER:
@@ -316,16 +355,26 @@
             remote(yts.at[t], yf.at[t, y, k], a_s.at[t, 0], a_r.at[t, k], partner).wait_send()
 
 
+def finish(sj_in, jj_in, sj_ref, jj_ref, sems):
+    copies = []
+    for j in range(2):
+        for i in range(4):
+            copies.append(pltpu.make_async_copy(sj_in.at[j, i], sj_ref.at[j, i], sems.at[j, i]))
+            r = slice(i * 128, i * 128 + 128)
+            copies.append(pltpu.make_async_copy(jj_in.at[j, r], jj_ref.at[j, r], sems.at[j, 4 + i]))
+    for copy in copies:
+        copy.start()
+    for copy in copies:
+        copy.wait()
+
+
 def local(sigma_anc, panel, pattern, linv):
-    row_ids = jnp.arange(4, dtype=jnp.int32) * 32 + lax.axis_index("row")
-    in_pattern = jnp.any(pattern[:, :, None] == row_ids[None, None, :], axis=1).astype(F32)
-    mask = jnp.broadcast_to(in_pattern[:, None, :, None], (2, 8, 4, 128)).reshape(2, 8, 512)
     s = sigma_anc.reshape(4, 4, 4, 128, 128)
     dma = pltpu.SemaphoreType.DMA
     vm = lambda *shape: pltpu.VMEM(shape, F32)
     vb = lambda *shape: pltpu.VMEM(shape, BF)
     pair = lambda *shape: [dma(shape), dma(shape)]
-    return pl.pallas_call(
+    results = pl.pallas_call(
         kernel,
         out_shape=(
             jax.ShapeDtypeStruct((2, 4, 128, 512), F32),
@@ -334,20 +383,28 @@
         in_specs=[pl.BlockSpec(memory_space=pl.ANY)] * 3 + [pl.BlockSpec(memory_space=pltpu.VMEM)],
         out_specs=[pl.BlockSpec(memory_space=pl.ANY)] * 2,
         scratch_shapes=[
-            vm(2, 512, 512), vm(2, 512, 512), vm(2, 4, 128, 512), vm(2, 512, 512),
+            vm(2, 8, 512), vm(2, 512, 512), vm(2, 512, 512), vm(2, 4, 128, 512), vm(2, 512, 512),
             vm(4, 4, 4, 128, 128), vm(4, 4, 4, 128, 128),
             vb(4, 2048, 512), vm(512, 512), vm(512, 512), vm(512, 512), vb(512, 2048), vb(2, 512, 512),
             vm(CH, 32, 512), vm(4, 512, 512), vm(CH, 2, 64, 512), vm(CH, 2, 128, 512),
             vm(CH, 4, 32, 512), vm(CH, 4, 32, 512), vm(CH, 32, 512), vm(CH, 4, 2, 32, 512),
             vm(CH, 32, 512), vm(CH, 4, 8, 512), vm(CH, 8, 8, 512),
-            dma((2, 2)), dma((CH, 3, 2)), dma((4,)), *pair(4), *pair(1), *pair(CH, 2), *pair(CH, 2), *pair(CH, 4), *pair(CH, 4),
+            dma((2, 2)), dma((CH, 3, 2)), dma((4,)), *pair(4), *pair(2), *pair(CH, 2), *pair(CH, 2), *pair(CH, 4), *pair(CH, 4),
             *pair(CH, 2), *pair(CH, 4), *pair(CH, 4), *pair(CH, 8), *pair(CH, 16), *pair(CH),
         ],
         compiler_params=pltpu.CompilerParams(
             collective_id=0, has_side_effects=True, vmem_limit_bytes=60 << 20
         ),
         name="selinv",
-    )(s, panel.reshape(2, 512, 512), linv, mask)
+    )(s, panel.reshape(2, 512, 512), linv, pattern)
+    return pl.pallas_call(
+        finish,
+        out_shape=tuple(jax.ShapeDtypeStruct(v.shape, F32) for v in results),
+        in_specs=[pl.BlockSpec(memory_space=pl.ANY)] * 2,
+        out_specs=[pl.BlockSpec(memory_space=pl.ANY)] * 2,
+        scratch_shapes=[dma((2, 8))],
+        name="finish",
+    )(*results)
 
 
 def solution(mesh):

time: 109 us -> 230 us (2.11)
  Pallas kernels: 102 us -> 229 us
  local copies, waits for them, and re-layouts: 5.25 us -> 0 us
    pallas_call x0 -> x1, Pallas kernels: none -> 128 us  [local(): pl.pallas_call(finish, out_shape=tuple((jax.ShapeDtypeStruct(v.shape, F32...]
    unnamed x6 -> x0, local copies, waits for them, and re-layouts: 4.63 us -> none
where the time goes in v3:
time: 230 us
  Pallas kernels  229 us (100%)
    pallas_call x1, Pallas kernels, local(): pl.pallas_call(finish, out_shape=tuple((jax.ShapeDtypeStruct(v.shape, F32...  128 us
    pallas_call x1, Pallas kernels, local(): pl.pallas_call(kernel, out_shape=(jax.ShapeDtypeStruct((2, 4, 128, 512),...  101 us

profile of v3, /device:TPU:1, one launch (start us, length us, event | category | flops | bytes accessed | tf_op | source)
XLA Modules:
  0.0 229.8 jit_solution(16298213079837857112)
XLA Ops:
  0.6 100.9 %selinv.1 = (f32[2,4,128,512]{3,2,1,0:T(8,128)}, f32[2,512,512]{2,1,0:T(8,128)}) custom-call(f32[4,4,4,128,128]{4,3,2,1,0:T(8,128)} %bitcast.2, f32[2,512,512]{2,1,0:T(8,128)} %bitcast.3, f32[2,512,512]{2,1,0:T(8,128)} %linv_ref.1, s32[2,64]{1,0:T(2,128)} %pattern_ref.1), custom_call_target="tpu_custom_call" | custom-call | tf_op jit(solution)/shard_map/selinv/pallas_call | solution.py:377
  101.5 128.3 %finish.1 = (f32[2,4,128,512]{3,2,1,0:T(8,128)}, f32[2,512,512]{2,1,0:T(8,128)}) custom-call(f32[2,4,128,512]{3,2,1,0:T(8,128)} %get-tuple-element.4.sj_in, f32[2,512,512]{2,1,0:T(8,128)} %get-tuple-element.5.jj_in), custom_call_target="tpu_custom_call" | custom-call | tf_op jit(solution)/shard_map/finish/pallas_call | solution.py:400

commit v4 on v2

--- a/solution.py
+++ b/solution.py
@@ -11,12 +11,12 @@
 CH = 4
 ORDER = (
     ("p", 0), ("o", 0), ("o", 1), ("p", 1), ("p", 2), ("b", 0), ("o", 2), ("b", 1),
-    ("o", 3), ("p", 3), ("v", 0), ("c", 0), ("b", 2), ("d", 0), ("b", 3), ("c", 1),
-    ("d", 1), ("e", 0), ("c", 2), ("d", 2), ("m", 0), ("e", 1), ("f", 0), ("c", 3),
-    ("d", 3), ("m", 1), ("e", 2), ("k", 0), ("g", 0), ("m", 2), ("f", 1), ("g", 1),
-    ("h", 0), ("l", 0), ("e", 3), ("f", 2), ("m", 3), ("k", 1), ("g", 2), ("h", 1),
-    ("l", 1), ("f", 3), ("g", 3), ("k", 2), ("h", 2), ("l", 2), ("h", 3), ("k", 3),
-    ("l", 3),
+    ("o", 3), ("p", 3), ("v", 0), ("b", 2), ("c", 0), ("b", 3), ("d", 0), ("c", 1),
+    ("d", 1), ("c", 2), ("e", 0), ("d", 2), ("c", 3), ("f", 0), ("e", 1), ("d", 3),
+    ("f", 1), ("e", 2), ("m", 0), ("m", 1), ("f", 2), ("e", 3), ("m", 2), ("g", 0),
+    ("f", 3), ("m", 3), ("g", 1), ("g", 2), ("i", 0), ("k", 0), ("g", 3), ("i", 1),
+    ("i", 2), ("k", 1), ("h", 0), ("i", 3), ("h", 1), ("l", 0), ("h", 2), ("k", 2),
+    ("l", 1), ("h", 3), ("l", 2), ("k", 3), ("l", 3),
 )
 NN = (((1,), (0,)), ((), ()))
 
@@ -32,8 +32,8 @@
 
 
 def kernel(
-    s_ref, panel_ref, linv_ref, mask_ref, sj_ref, jj_ref,
-    pbuf, lbuf, sjv, jjv, so, sp, scat, uto, uts, utp, ucat, gu, bs,
+    s_ref, panel_ref, linv_ref, pattern_ref, sj_ref, jj_ref,
+    mask_ref, pbuf, lbuf, sjv, jjv, so, sp, scat, uto, uts, utp, ucat, gu, bs,
     tt, ol, nl, yl, zl_, yts, yf, gs, gx, gzl,
     in_s, out_s, s_loc, s_s, s_r, u_s, u_r, o_s, o_r, n_s, n_r, y_s, y_r, z_s, z_r,
     a_s, a_r, b_s, b_r, gx_s, gx_r, gz_s, gz_r, gb_s, gb_r, gd_s, gd_r,
@@ -65,7 +65,7 @@
     cross = dev(x, y, zh, 1 - zl, other)
     peers = [partner, cross]
     peers += [at_z(d) for d in range(1, 8)]
-    peers += [dev((x + n // 4) % 4, (y + n % 4) % 4, zh, zl, k) for n in range(1, 16)]
+    peers += [at_x(d) for d in (1, 2, 3)] + [at_y(d) for d in (1, 2, 3)]
 
     sent, outs = [], []
 
@@ -99,6 +99,13 @@
         copy = pltpu.make_async_copy(s_ref.at[:, :, (x + offs[p]) % 4], so.at[p], s_loc.at[p])
         copy.start()
         local.append(copy)
+
+    pattern = pattern_ref[...]
+    for i in range(4):
+        hit = jnp.where(pattern == i * 32 + row, 1.0, 0.0).astype(F32)
+        for j in range(2):
+            value = jnp.max(hit[j : j + 1], axis=1, keepdims=True)
+            mask_ref[j, :, i * 128 : (i + 1) * 128] = jnp.broadcast_to(value, (8, 128))
 
     def update(j):
         a = split(pbuf[j])
@@ -246,12 +253,18 @@
             g = g + gzl[t, q, :, c]
         r = tile_row(t, x, y)
         jjv[k, r, c] = g
-        for n in range(1, 16):
-            dx, dy = n // 4, n % 4
-            push(
-                jjv.at[k, r, c], jjv.at[k, r, c], gb_s.at[t, n], gb_r.at[t, x * 4 + y],
-                dev((x + dx) % 4, (y + dy) % 4, zh, zl, k),
-            )
+        for d in (1, 2, 3):
+            push(jjv.at[k, r, c], jjv.at[k, r, c], gb_s.at[t, d], gb_r.at[t, x * 4 + y], at_y(d))
+
+    def phase_i(t):
+        c = slice(t * 128, 512)
+        for dy in range(4):
+            q = (y + dy) % 4
+            r = tile_row(t, x, q)
+            if dy:
+                arrived(jjv.at[k, r, c], gb_s.at[t, dy], gb_r.at[t, x * 4 + q])
+            for dx in (1, 2, 3):
+                push(jjv.at[k, r, c], jjv.at[k, r, c], gb_s.at[t, dx * 4 + dy], gb_r.at[t, x * 4 + q], at_x(dx))
 
     def store(t, j, side):
         r, c = slice(t * 128, t * 128 + 128), slice(t * 128, 512)
@@ -269,7 +282,7 @@
 
     def phase_h(t):
         r, c = slice(t * 128, t * 128 + 128), slice(t * 128, 512)
-        for n in range(1, 16):
+        for n in range(4, 16):
             dx, dy = n // 4, n % 4
             qx, qy = (x + dx) % 4, (y + dy) % 4
             arrived(jjv.at[k, tile_row(t, qx, qy), c], gb_s.at[t, n], gb_r.at[t, qx * 4 + qy])
@@ -299,7 +312,7 @@
                 store(t, j, 1)
 
     phases = dict(
-        o=phase_o, p=phase_p, v=phase_v, b=phase_b, c=phase_c, d=phase_d, e=phase_e, f=phase_f, g=phase_g,
+        o=phase_o, p=phase_p, i=phase_i, v=phase_v, b=phase_b, c=phase_c, d=phase_d, e=phase_e, f=phase_f, g=phase_g,
         h=phase_h, k=phase_k, l=phase_l, m=phase_m,
     )
     for name, t in ORDER:
@@ -316,16 +329,31 @@
             remote(yts.at[t], yf.at[t, y, k], a_s.at[t, 0], a_r.at[t, k], partner).wait_send()
 
 
+def finish(sj_in, jj_in, sj_ref, jj_ref, sj_buf, jj_buf, in_s, out_s):
+    parts = []
+    for j in range(2):
+        for i in range(4):
+            parts.append((sj_in.at[j, i], sj_buf.at[j, i], sj_ref.at[j, i], (j, i)))
+            r = slice(i * 128, i * 128 + 128)
+            parts.append((jj_in.at[j, r], jj_buf.at[j, r], jj_ref.at[j, r], (j, 4 + i)))
+    loads = [pltpu.make_async_copy(a, b, in_s.at[n]) for a, b, c, n in parts]
+    stores = [pltpu.make_async_copy(b, c, out_s.at[n]) for a, b, c, n in parts]
+    for copy in loads:
+        copy.start()
+    for load, store in zip(loads, stores):
+        load.wait()
+        store.start()
+    for copy in stores:
+        copy.wait()
+
+
 def local(sigma_anc, panel, pattern, linv):
-    row_ids = jnp.arange(4, dtype=jnp.int32) * 32 + lax.axis_index("row")
-    in_pattern = jnp.any(pattern[:, :, None] == row_ids[None, None, :], axis=1).astype(F32)
-    mask = jnp.broadcast_to(in_pattern[:, None, :, None], (2, 8, 4, 128)).reshape(2, 8, 512)
     s = sigma_anc.reshape(4, 4, 4, 128, 128)
     dma = pltpu.SemaphoreType.DMA
     vm = lambda *shape: pltpu.VMEM(shape, F32)
     vb = lambda *shape: pltpu.VMEM(shape, BF)
     pair = lambda *shape: [dma(shape), dma(shape)]
-    return pl.pallas_call(
+    results = pl.pallas_call(
         kernel,
         out_shape=(
             jax.ShapeDtypeStruct((2, 4, 128, 512), F32),
@@ -334,7 +362,7 @@
         in_specs=[pl.BlockSpec(memory_space=pl.ANY)] * 3 + [pl.BlockSpec(memory_space=pltpu.VMEM)],
         out_specs=[pl.BlockSpec(memory_space=pl.ANY)] * 2,
         scratch_shapes=[
-            vm(2, 512, 512), vm(2, 512, 512), vm(2, 4, 128, 512), vm(2, 512, 512),
+            vm(2, 8, 512), vm(2, 512, 512), vm(2, 512, 512), vm(2, 4, 128, 512), vm(2, 512, 512),
             vm(4, 4, 4, 128, 128), vm(4, 4, 4, 128, 128),
             vb(4, 2048, 512), vm(512, 512), vm(512, 512), vm(512, 512), vb(512, 2048), vb(2, 512, 512),
             vm(CH, 32, 512), vm(4, 512, 512), vm(CH, 2, 64, 512), vm(CH, 2, 128, 512),
@@ -347,7 +375,15 @@
             collective_id=0, has_side_effects=True, vmem_limit_bytes=60 << 20
         ),
         name="selinv",
-    )(s, panel.reshape(2, 512, 512), linv, mask)
+    )(s, panel.reshape(2, 512, 512), linv, pattern)
+    return pl.pallas_call(
+        finish,
+        out_shape=tuple(jax.ShapeDtypeStruct(v.shape, F32) for v in results),
+        in_specs=[pl.BlockSpec(memory_space=pl.ANY)] * 2,
+        out_specs=[pl.BlockSpec(memory_space=pl.ANY)] * 2,
+        scratch_shapes=[vm(2, 4, 128, 512), vm(2, 512, 512), dma((2, 8)), dma((2, 8))],
+        name="finish",
+    )(*results)
 
 
 def solution(mesh):

time: 109 us -> 101 us (0.927)
  local copies, waits for them, and re-layouts: 5.25 us -> 0 us
  Pallas kernels: 102 us -> 99.8 us
    pallas_call x1, Pallas kernels: 102 us -> 96 us  [local(): pl.pallas_call(kernel, out_shape=(jax.ShapeDtypeStruct((2, 4, 128, 512),...]
    unnamed x6 -> x0, local copies, waits for them, and re-layouts: 4.63 us -> none
    pallas_call x0 -> x1, Pallas kernels: none -> 3.85 us  [local(): pl.pallas_call(finish, out_shape=tuple((jax.ShapeDtypeStruct(v.shape, F32...]
where the time goes in v4:
time: 101 us; the launch traced here: 100 us
  Pallas kernels  99.8 us (99%)
    pallas_call x1, Pallas kernels, local(): pl.pallas_call(kernel, out_shape=(jax.ShapeDtypeStruct((2, 4, 128, 512),...  96 us
    pallas_call x1, Pallas kernels, local(): pl.pallas_call(finish, out_shape=tuple((jax.ShapeDtypeStruct(v.shape, F32...  3.85 us

profile of v4, /device:TPU:1, one launch (start us, length us, event | category | flops | bytes accessed | tf_op | source)
XLA Modules:
  0.0 100.5 jit_solution(6055249374353909442)
XLA Ops:
  0.6 96.0 %selinv.1 = (f32[2,4,128,512]{3,2,1,0:T(8,128)}, f32[2,512,512]{2,1,0:T(8,128)}) custom-call(f32[4,4,4,128,128]{4,3,2,1,0:T(8,128)} %bitcast.2, f32[2,512,512]{2,1,0:T(8,128)} %bitcast.3, f32[2,512,512]{2,1,0:T(8,128)} %linv_ref.1, s32[2,64]{1,0:T(2,128)} %pattern_ref.1), custom_call_target="tpu_custom_call" | custom-call | tf_op jit(solution)/shard_map/selinv/pallas_call | solution.py:356
  96.6 3.9 %finish.1 = (f32[2,4,128,512]{3,2,1,0:T(8,128)}, f32[2,512,512]{2,1,0:T(8,128)}) custom-call(f32[2,4,128,512]{3,2,1,0:T(8,128)} %get-tuple-element.4.sj_in, f32[2,512,512]{2,1,0:T(8,128)} %get-tuple-element.5.jj_in), custom_call_target="tpu_custom_call" | custom-call | tf_op jit(solution)/shard_map/finish/pallas_call | solution.py:379

commit v5 on v4

--- a/solution.py
+++ b/solution.py
@@ -13,10 +13,9 @@
     ("p", 0), ("o", 0), ("o", 1), ("p", 1), ("p", 2), ("b", 0), ("o", 2), ("b", 1),
     ("o", 3), ("p", 3), ("v", 0), ("b", 2), ("c", 0), ("b", 3), ("d", 0), ("c", 1),
     ("d", 1), ("c", 2), ("e", 0), ("d", 2), ("c", 3), ("f", 0), ("e", 1), ("d", 3),
-    ("f", 1), ("e", 2), ("m", 0), ("m", 1), ("f", 2), ("e", 3), ("m", 2), ("g", 0),
-    ("f", 3), ("m", 3), ("g", 1), ("g", 2), ("i", 0), ("k", 0), ("g", 3), ("i", 1),
-    ("i", 2), ("k", 1), ("h", 0), ("i", 3), ("h", 1), ("l", 0), ("h", 2), ("k", 2),
-    ("l", 1), ("h", 3), ("l", 2), ("k", 3), ("l", 3),
+    ("f", 1), ("e", 2), ("m", 0), ("f", 2), ("e", 3), ("g", 0), ("m", 1), ("f", 3),
+    ("i", 0), ("g", 1), ("k", 0), ("k", 1), ("h", 0), ("i", 1), ("k", 2), ("l", 0),
+    ("h", 1), ("k", 3), ("l", 1),
 )
 NN = (((1,), (0,)), ((), ()))
 
@@ -212,13 +211,14 @@
 
         push(yts.at[t], yf.at[t, y, k], a_s.at[t, 1], a_r.at[t, k], dev(x, y, zh, 1 - zl, zl))
         yh, yl_ = split(yt)
-        c = slice(t * 128, 512)
+        b = t // 2
+        c = slice(b * 256, 512)
         g = jnp.dot(jnp.concatenate([yh, yl_]), gu[0, :, c], preferred_element_type=F32)
         g2 = jnp.dot(yh, gu[1, :, c], preferred_element_type=F32)
         gs[t, :, c] = (g[0:32] + bs[t, :, c]) + (g[32:64] + g2)
-        for d in (1, 2, 3):
+        for d in (1, 2, 3) if t % 2 else ():
             r = pl.ds(pl.multiple_of((x + d) % 4 * 8, 8), 8)
-            push(gs.at[t, r, c], gx.at[t, x, :, c], gx_s.at[t, d], gx_r.at[t, x], at_x(d))
+            push(gs.at[t - 1 : t + 1, r, c], gx.at[b, x, :, :, c], gx_s.at[b, d], gx_r.at[b, x], at_x(d))
 
     def phase_f(t):
         arrived(yf.at[t, y, other], a_s.at[t, 0], a_r.at[t, other])
@@ -229,64 +229,66 @@
 
         for d in (1, 2, 3):
             push(yf.at[t, y], yf.at[t, y], b_s.at[t, d], b_r.at[t, y], at_y(d))
-    def phase_m(t):
-        c = slice(t * 128, 512)
+    def phase_m(b):
+        t, c = slice(b * 2, b * 2 + 2), slice(b * 256, 512)
         g = gs[t, pl.ds(pl.multiple_of(x * 8, 8), 8), c]
         for d in (1, 2, 3):
             q = (x + d) % 4
-            arrived(gx.at[t, q, :, c], gx_s.at[t, d], gx_r.at[t, q])
-            g = g + gx[t, q, :, c]
-        gzl[t, z, :, c] = g
+            arrived(gx.at[b, q, :, :, c], gx_s.at[b, d], gx_r.at[b, q])
+            g = g + gx[b, q, :, :, c]
+        gzl[b, z, :, :, c] = g
         for d in range(1, 8):
-            push(gzl.at[t, z, :, c], gzl.at[t, z, :, c], gz_s.at[t, d], gz_r.at[t, z], at_z(d))
-
-    def tile_row(t, x, y):
-        return pl.ds(pl.multiple_of(t * 128 + y * 32 + x * 8, 8), 8)
-
-    def phase_g(t):
-        c = slice(t * 128, 512)
+            push(gzl.at[b, z, :, :, c], gzl.at[b, z, :, :, c], gz_s.at[b, d], gz_r.at[b, z], at_z(d))
+
+    def piece(b, x, y):
+        r = pl.ds(pl.multiple_of(y * 32 + x * 8, 8), 8)
+        return jjv.at[k, b * 2 : b * 2 + 2, r, b * 256 : 512]
+
+    def phase_g(b):
+        t, c = slice(b * 2, b * 2 + 2), slice(b * 256, 512)
         for d in range(1, 8):
             q = (z + d) % 8
-            arrived(gzl.at[t, q, :, c], gz_s.at[t, d], gz_r.at[t, q])
-        g = gzl[t, 0, :, c]
+            arrived(gzl.at[b, q, :, :, c], gz_s.at[b, d], gz_r.at[b, q])
+        g = gzl[b, 0, :, :, c]
         for q in range(1, 8):
-            g = g + gzl[t, q, :, c]
-        r = tile_row(t, x, y)
-        jjv[k, r, c] = g
-        for d in (1, 2, 3):
-            push(jjv.at[k, r, c], jjv.at[k, r, c], gb_s.at[t, d], gb_r.at[t, x * 4 + y], at_y(d))
-
-    def phase_i(t):
-        c = slice(t * 128, 512)
+            g = g + gzl[b, q, :, :, c]
+        jjv[k, t, pl.ds(pl.multiple_of(y * 32 + x * 8, 8), 8), c] = g
+        for d in (1, 2, 3):
+            push(piece(b, x, y), piece(b, x, y), gb_s.at[b, d], gb_r.at[b, x * 4 + y], at_y(d))
+
+    def phase_i(b):
         for dy in range(4):
             q = (y + dy) % 4
-            r = tile_row(t, x, q)
+            part = piece(b, x, q)
             if dy:
-                arrived(jjv.at[k, r, c], gb_s.at[t, dy], gb_r.at[t, x * 4 + q])
+                arrived(part, gb_s.at[b, dy], gb_r.at[b, x * 4 + q])
             for dx in (1, 2, 3):
-                push(jjv.at[k, r, c], jjv.at[k, r, c], gb_s.at[t, dx * 4 + dy], gb_r.at[t, x * 4 + q], at_x(dx))
-
-    def store(t, j, side):
-        r, c = slice(t * 128, t * 128 + 128), slice(t * 128, 512)
-        if side:
-            r, c = slice(t * 128 + 128, 512), r
-        copy = pltpu.make_async_copy(jjv.at[j, r, c], jj_ref.at[j, r, c], out_s.at[t, side, j])
-        copy.start()
-        outs.append(copy)
-
-    def mirror(t, j):
-        r = slice(t * 128, t * 128 + 128)
-        for n in range(t + 1, 4):
-            c = slice(n * 128, n * 128 + 128)
-            jjv[j, c, r] = jjv[j, r, c].T
-
-    def phase_h(t):
-        r, c = slice(t * 128, t * 128 + 128), slice(t * 128, 512)
+                push(part, part, gb_s.at[b, dx * 4 + dy], gb_r.at[b, x * 4 + q], at_x(dx))
+
+    def phase_h(b):
         for n in range(4, 16):
             dx, dy = n // 4, n % 4
             qx, qy = (x + dx) % 4, (y + dy) % 4
-            arrived(jjv.at[k, tile_row(t, qx, qy), c], gb_s.at[t, n], gb_r.at[t, qx * 4 + qy])
-        push(jjv.at[k, r, c], jjv.at[k, r, c], gd_s.at[t], gd_r.at[t], partner)
+            arrived(piece(b, qx, qy), gb_s.at[b, n], gb_r.at[b, qx * 4 + qy])
+        part = jjv.at[k, b * 2 : b * 2 + 2, :, b * 256 : 512]
+        push(part, part, gd_s.at[b], gd_r.at[b], partner)
+
+    def store(j, t, c, sem):
+        copy = pltpu.make_async_copy(jjv.at[j, t, :, c], jj_ref.at[j, t, :, c], sem)
+        copy.start()
+        outs.append(copy)
+
+    def phase_l(b):
+        t, c = slice(b * 2, b * 2 + 2), slice(b * 256, 512)
+        arrived(jjv.at[other, t, :, c], gd_s.at[b], gd_r.at[b])
+        for j in range(2):
+            store(j, t, c, out_s.at[b, 0, j])
+            if b == 0:
+                for n in (2, 3):
+                    for m in (0, 1):
+                        block = jjv[j, m, :, n * 128 : n * 128 + 128]
+                        jjv[j, n, :, m * 128 : m * 128 + 128] = block.T
+                store(j, slice(2, 4), slice(0, 256), out_s.at[b, 1, j])
 
     def phase_k(t):
         for d in (1, 2, 3):
@@ -302,15 +304,6 @@
         copy.start()
         outs.append(copy)
 
-    def phase_l(t):
-        r, c = slice(t * 128, t * 128 + 128), slice(t * 128, 512)
-        arrived(jjv.at[other, r, c], gd_s.at[t], gd_r.at[t])
-        for j in range(2):
-            store(t, j, 0)
-            if t < 3:
-                mirror(t, j)
-                store(t, j, 1)
-
     phases = dict(
         o=phase_o, p=phase_p, i=phase_i, v=phase_v, b=phase_b, c=phase_c, d=phase_d, e=phase_e, f=phase_f, g=phase_g,
         h=phase_h, k=phase_k, l=phase_l, m=phase_m,
@@ -332,10 +325,8 @@
 def finish(sj_in, jj_in, sj_ref, jj_ref, sj_buf, jj_buf, in_s, out_s):
     parts = []
     for j in range(2):
-        for i in range(4):
-            parts.append((sj_in.at[j, i], sj_buf.at[j, i], sj_ref.at[j, i], (j, i)))
-            r = slice(i * 128, i * 128 + 128)
-            parts.append((jj_in.at[j, r], jj_buf.at[j, r], jj_ref.at[j, r], (j, 4 + i)))
+        parts.append((sj_in.at[j], sj_buf.at[j], sj_ref.at[j], (0, j)))
+        parts.append((jj_in.at[j], jj_buf.at[j], jj_ref.at[j], (1, j)))
     loads = [pltpu.make_async_copy(a, b, in_s.at[n]) for a, b, c, n in parts]
     stores = [pltpu.make_async_copy(b, c, out_s.at[n]) for a, b, c, n in parts]
     for copy in loads:
@@ -357,33 +348,34 @@
         kernel,
         out_shape=(
             jax.ShapeDtypeStruct((2, 4, 128, 512), F32),
-            jax.ShapeDtypeStruct((2, 512, 512), F32),
+            jax.ShapeDtypeStruct((2, 4, 128, 512), F32),
         ),
         in_specs=[pl.BlockSpec(memory_space=pl.ANY)] * 3 + [pl.BlockSpec(memory_space=pltpu.VMEM)],
         out_specs=[pl.BlockSpec(memory_space=pl.ANY)] * 2,
         scratch_shapes=[
-            vm(2, 8, 512), vm(2, 512, 512), vm(2, 512, 512), vm(2, 4, 128, 512), vm(2, 512, 512),
+            vm(2, 8, 512), vm(2, 512, 512), vm(2, 512, 512), vm(2, 4, 128, 512), vm(2, 4, 128, 512),
             vm(4, 4, 4, 128, 128), vm(4, 4, 4, 128, 128),
             vb(4, 2048, 512), vm(512, 512), vm(512, 512), vm(512, 512), vb(512, 2048), vb(2, 512, 512),
             vm(CH, 32, 512), vm(4, 512, 512), vm(CH, 2, 64, 512), vm(CH, 2, 128, 512),
             vm(CH, 4, 32, 512), vm(CH, 4, 32, 512), vm(CH, 32, 512), vm(CH, 4, 2, 32, 512),
-            vm(CH, 32, 512), vm(CH, 4, 8, 512), vm(CH, 8, 8, 512),
+            vm(CH, 32, 512), vm(2, 4, 2, 8, 512), vm(2, 8, 2, 8, 512),
             dma((2, 2)), dma((CH, 3, 2)), dma((4,)), *pair(4), *pair(1), *pair(CH, 2), *pair(CH, 2), *pair(CH, 4), *pair(CH, 4),
-            *pair(CH, 2), *pair(CH, 4), *pair(CH, 4), *pair(CH, 8), *pair(CH, 16), *pair(CH),
+            *pair(CH, 2), *pair(CH, 4), *pair(2, 4), *pair(2, 8), *pair(2, 16), *pair(2),
         ],
         compiler_params=pltpu.CompilerParams(
             collective_id=0, has_side_effects=True, vmem_limit_bytes=60 << 20
         ),
         name="selinv",
     )(s, panel.reshape(2, 512, 512), linv, pattern)
-    return pl.pallas_call(
+    sj, jj = pl.pallas_call(
         finish,
         out_shape=tuple(jax.ShapeDtypeStruct(v.shape, F32) for v in results),
         in_specs=[pl.BlockSpec(memory_space=pl.ANY)] * 2,
         out_specs=[pl.BlockSpec(memory_space=pl.ANY)] * 2,
-        scratch_shapes=[vm(2, 4, 128, 512), vm(2, 512, 512), dma((2, 8)), dma((2, 8))],
+        scratch_shapes=[vm(2, 4, 128, 512), vm(2, 4, 128, 512), dma((2, 2)), dma((2, 2))],
         name="finish",
     )(*results)
+    return sj, jj.reshape(2, 512, 512)
 
 
 def solution(mesh):

time: 101 us -> 102 us (level)
  Pallas kernels: 99.8 us -> 101 us
    pallas_call x1, Pallas kernels: 96 us -> 97.4 us  [local(): pl.pallas_call(kernel, out_shape=(jax.ShapeDtypeStruct((2, 4, 128, 512),...]
where the time goes in v5:
time: 102 us; the launch traced here: 101 us
  Pallas kernels  101 us (99%)
    pallas_call x1, Pallas kernels, local(): pl.pallas_call(kernel, out_shape=(jax.ShapeDtypeStruct((2, 4, 128, 512),...  97.4 us
    pallas_call x1, Pallas kernels, local(): pl.pallas_call(finish, out_shape=tuple((jax.ShapeDtypeStruct(v.shape, F32...  3.3 us

profile of v5, /device:TPU:1, one launch (start us, length us, event | category | flops | bytes accessed | tf_op | source)
XLA Modules:
  0.0 101.4 jit_solution(16632625988671398527)
XLA Ops:
  0.6 97.4 %selinv.1 = (f32[2,4,128,512]{3,2,1,0:T(8,128)}, f32[2,4,128,512]{3,2,1,0:T(8,128)}) custom-call(f32[4,4,4,128,128]{4,3,2,1,0:T(8,128)} %bitcast.3, f32[2,512,512]{2,1,0:T(8,128)} %bitcast.4, f32[2,512,512]{2,1,0:T(8,128)} %linv_ref.1, s32[2,64]{1,0:T(2,128)} %pattern_ref.1), custom_call_target="tpu_custom_call" | custom-call | tf_op jit(solution)/shard_map/selinv/pallas_call | solution.py:347
  98.1 3.3 %finish.1 = (f32[2,4,128,512]{3,2,1,0:T(8,128)}, f32[2,4,128,512]{3,2,1,0:T(8,128)}) custom-call(f32[2,4,128,512]{3,2,1,0:T(8,128)} %get-tuple-element.6.sj_in, f32[2,4,128,512]{3,2,1,0:T(8,128)} %get-tuple-element.7.jj_in), custom_call_target="tpu_custom_call" | custom-call | tf_op jit(solution)/shard_map/finish/pallas_call | solution.py:370

commit v6 on v4

--- a/solution.py
+++ b/solution.py
@@ -10,8 +10,8 @@
 F32 = jnp.float32
 CH = 4
 ORDER = (
-    ("p", 0), ("o", 0), ("o", 1), ("p", 1), ("p", 2), ("b", 0), ("o", 2), ("b", 1),
-    ("o", 3), ("p", 3), ("v", 0), ("b", 2), ("c", 0), ("b", 3), ("d", 0), ("c", 1),
+    ("p", 0), ("o", 0), ("o", 1), ("o", 2), ("p", 1), ("p", 2), ("b", 0), ("o", 3),
+    ("b", 1), ("p", 3), ("c", 0), ("b", 2), ("v", 0), ("b", 3), ("d", 0), ("c", 1),
     ("d", 1), ("c", 2), ("e", 0), ("d", 2), ("c", 3), ("f", 0), ("e", 1), ("d", 3),
     ("f", 1), ("e", 2), ("m", 0), ("m", 1), ("f", 2), ("e", 3), ("m", 2), ("g", 0),
     ("f", 3), ("m", 3), ("g", 1), ("g", 2), ("i", 0), ("k", 0), ("g", 3), ("i", 1),
@@ -332,10 +332,8 @@
 def finish(sj_in, jj_in, sj_ref, jj_ref, sj_buf, jj_buf, in_s, out_s):
     parts = []
     for j in range(2):
-        for i in range(4):
-            parts.append((sj_in.at[j, i], sj_buf.at[j, i], sj_ref.at[j, i], (j, i)))
-            r = slice(i * 128, i * 128 + 128)
-            parts.append((jj_in.at[j, r], jj_buf.at[j, r], jj_ref.at[j, r], (j, 4 + i)))
+        parts.append((sj_in.at[j], sj_buf.at[j], sj_ref.at[j], (0, j)))
+        parts.append((jj_in.at[j], jj_buf.at[j], jj_ref.at[j], (1, j)))
     loads = [pltpu.make_async_copy(a, b, in_s.at[n]) for a, b, c, n in parts]
     stores = [pltpu.make_async_copy(b, c, out_s.at[n]) for a, b, c, n in parts]
     for copy in loads:
@@ -381,7 +379,7 @@
         out_shape=tuple(jax.ShapeDtypeStruct(v.shape, F32) for v in results),
         in_specs=[pl.BlockSpec(memory_space=pl.ANY)] * 2,
         out_specs=[pl.BlockSpec(memory_space=pl.ANY)] * 2,
-        scratch_shapes=[vm(2, 4, 128, 512), vm(2, 512, 512), dma((2, 8)), dma((2, 8))],
+        scratch_shapes=[vm(2, 4, 128, 512), vm(2, 512, 512), dma((2, 2)), dma((2, 2))],
         name="finish",
     )(*results)
 

time: 101 us -> 99.1 us (0.981)
  Pallas kernels: 99.8 us -> 98.4 us
where the time goes in v6:
time: 99.1 us; the launch traced here: 99 us
  Pallas kernels  98.4 us (99%)
    pallas_call x1, Pallas kernels, local(): pl.pallas_call(kernel, out_shape=(jax.ShapeDtypeStruct((2, 4, 128, 512),...  95.1 us
    pallas_call x1, Pallas kernels, local(): pl.pallas_call(finish, out_shape=tuple((jax.ShapeDtypeStruct(v.shape, F32...  3.3 us

profile of v6, /device:TPU:1, one launch (start us, length us, event | category | flops | bytes accessed | tf_op | source)
XLA Modules:
  0.0 99.0 jit_solution(12700612633258595021)
XLA Ops:
  0.6 95.1 %selinv.1 = (f32[2,4,128,512]{3,2,1,0:T(8,128)}, f32[2,512,512]{2,1,0:T(8,128)}) custom-call(f32[4,4,4,128,128]{4,3,2,1,0:T(8,128)} %bitcast.2, f32[2,512,512]{2,1,0:T(8,128)} %bitcast.3, f32[2,512,512]{2,1,0:T(8,128)} %linv_ref.1, s32[2,64]{1,0:T(2,128)} %pattern_ref.1), custom_call_target="tpu_custom_call" | custom-call | tf_op jit(solution)/shard_map/selinv/pallas_call | solution.py:354
  95.7 3.3 %finish.1 = (f32[2,4,128,512]{3,2,1,0:T(8,128)}, f32[2,512,512]{2,1,0:T(8,128)}) custom-call(f32[2,4,128,512]{3,2,1,0:T(8,128)} %get-tuple-element.4.sj_in, f32[2,512,512]{2,1,0:T(8,128)} %get-tuple-element.5.jj_in), custom_call_target="tpu_custom_call" | custom-call | tf_op jit(solution)/shard_map/finish/pallas_call | solution.py:377

commit v7 on v6

--- a/solution.py
+++ b/solution.py
@@ -86,19 +86,19 @@
     for peer in peers:
         pl.semaphore_signal(barrier, inc=1, device_id=peer, device_id_type=MESH)
 
+    offs = (2, 1, 3, 0)
+    local = []
+    for p in range(4):
+        copy = pltpu.make_async_copy(s_ref.at[:, :, (x + offs[p]) % 4], so.at[p], s_loc.at[p])
+        copy.start()
+        local.append(copy)
+
     loads = []
     for n, j in enumerate((other, k)):
         for m, (src, dst) in enumerate(((panel_ref, pbuf), (linv_ref, lbuf))):
             copy = pltpu.make_async_copy(src.at[j], dst.at[j], in_s.at[n, m])
             copy.start()
             loads.append(copy)
-
-    offs = (2, 1, 3, 0)
-    local = []
-    for p in range(4):
-        copy = pltpu.make_async_copy(s_ref.at[:, :, (x + offs[p]) % 4], so.at[p], s_loc.at[p])
-        copy.start()
-        local.append(copy)
 
     pattern = pattern_ref[...]
     for i in range(4):

time: 99.1 us -> 99.9 us (level)
  no operation moved by 1% of the time
where the time goes in v7:
time: 99.9 us; the launch traced here: 99.8 us
  Pallas kernels  99.1 us (99%)
    pallas_call x1, Pallas kernels, local(): pl.pallas_call(kernel, out_shape=(jax.ShapeDtypeStruct((2, 4, 128, 512),...  95.8 us
    pallas_call x1, Pallas kernels, local(): pl.pallas_call(finish, out_shape=tuple((jax.ShapeDtypeStruct(v.shape, F32...  3.3 us

profile of v7, /device:TPU:1, one launch (start us, length us, event | category | flops | bytes accessed | tf_op | source)
XLA Modules:
  0.0 99.8 jit_solution(18398882285415932810)
XLA Ops:
  0.6 95.8 %selinv.1 = (f32[2,4,128,512]{3,2,1,0:T(8,128)}, f32[2,512,512]{2,1,0:T(8,128)}) custom-call(f32[4,4,4,128,128]{4,3,2,1,0:T(8,128)} %bitcast.2, f32[2,512,512]{2,1,0:T(8,128)} %bitcast.3, f32[2,512,512]{2,1,0:T(8,128)} %linv_ref.1, s32[2,64]{1,0:T(2,128)} %pattern_ref.1), custom_call_target="tpu_custom_call" | custom-call | tf_op jit(solution)/shard_map/selinv/pallas_call | solution.py:354
  96.5 3.3 %finish.1 = (f32[2,4,128,512]{3,2,1,0:T(8,128)}, f32[2,512,512]{2,1,0:T(8,128)}) custom-call(f32[2,4,128,512]{3,2,1,0:T(8,128)} %get-tuple-element.4.sj_in, f32[2,512,512]{2,1,0:T(8,128)} %get-tuple-element.5.jj_in), custom_call_target="tpu_custom_call" | custom-call | tf_op jit(solution)/shard_map/finish/pallas_call | solution.py:377
